TPU v7x, 256 devices: a whole 4x4x8 slice. The times are simulated.
256 devices in a mesh: gx: 32 (over y, z_lo, x), gy: 8 (over z_hi, core).
Axes of the slice: x: 4, y: 4, z: 8 (z_hi: 4, z_lo: 2; z = z_hi * 2 + z_lo), core: 2. Of those that a mesh axis runs over, the one named last changes fastest.
Arguments:
- hidden: bfloat16 [2240, 5120], P('gy', 'gx'), may hold values from -6 to 6
- norm_gain: float32 [5120], P('gx'), may hold values from 0.1 to 1.9
- qkv_weight: bfloat16 [5120, 7168], P('gx', 'gy'), may hold values from -0.078125 to 0.078125
- qkv_bias: bfloat16 [7168], P('gy'), may hold values from -5 to 5
- out_weight: bfloat16 [5120, 5120], P('gy', 'gx'), may hold values from -0.078125 to 0.078125
- key_cache: bfloat16 [5, 8704, 1024], P(None, 'gx', 'gy'), may hold values from -68 to 68
- value_cache: bfloat16 [5, 8704, 1024], P(None, 'gx', 'gy'), may hold values from -12 to 12
- cached_len: int32 [5], replicated, may hold values from 1 to 8192, as said below
- fresh_len: int32 [5], replicated, may hold values from 224 to 448, as said below
Outputs:
- output: bfloat16 [2240, 5120], P('gy', 'gx')
- key_out: bfloat16 [5, 8704, 1024], P(None, 'gx', 'gy')
- value_out: bfloat16 [5, 8704, 1024], P(None, 'gx', 'gy')
Inputs may be any that keep to these rules, and one draw needn't show every extreme that they name: `cached_len`: two requests have 8192 - 8192 // 32 or more cached tokens, one of them exactly 8192; the other three fewer than 256. `fresh_len`: one request has exactly 448 live new tokens.
All inputs are finite; a program needn't handle non-finite values.
Results may differ from a plain program's by a relative error of at most 0.012.
Values may be sent and summed in bfloat16 or wider, within the bound.
A program may use at most 128 MiB of HBM per device.

v0:
```python
import jax
import jax.numpy as jnp
from jax import lax
from jax.sharding import Mesh
from jax.sharding import PartitionSpec as P

HEAD_DIM = 128
GROUP = 5
REQUESTS = 5
NEW_TOKENS = 448
ROPE_THETA = 1000000.0
NORM_EPS = 1e-06
NEG_LARGE = -1e30


def rotate(vectors, positions):
    half_dim = vectors.shape[-1] // 2
    exponent = jnp.arange(half_dim, dtype=jnp.int32).astype(jnp.float32) * (2.0 / vectors.shape[-1])
    frequency = 1.0 / ROPE_THETA**exponent
    angles = positions[:, None] * frequency[None, :]
    target = (positions.shape[0],) + (1,) * (vectors.ndim - 2) + (half_dim,)
    cos_table = jnp.cos(angles).reshape(target)
    sin_table = jnp.sin(angles).reshape(target)
    first_half = vectors[..., :half_dim]
    second_half = vectors[..., half_dim:]
    return jnp.concatenate(
        [
            first_half * cos_table - second_half * sin_table,
            second_half * cos_table + first_half * sin_table,
        ],
        -1,
    )


def token_positions(cached_len, fresh_len, first_row, row_count):
    rows_here = first_row + jnp.arange(row_count, dtype=jnp.int32)
    request = rows_here // NEW_TOKENS
    within = rows_here % NEW_TOKENS
    picked = request[:, None] == jnp.arange(REQUESTS, dtype=jnp.int32)[None, :]
    start_pos = jnp.sum(jnp.where(picked, cached_len[None, :], 0), 1)
    live_count = jnp.sum(jnp.where(picked, fresh_len[None, :], 0), 1)
    return (start_pos + within, within < live_count)


def finish_rows(projected, cached_len, fresh_len, first_row):
    row_count = projected.shape[0]
    groups_here = projected.shape[1] // ((GROUP + 2) * HEAD_DIM)
    shaped = projected.reshape(row_count, groups_here, GROUP + 2, HEAD_DIM)
    positions, unused_live = token_positions(cached_len, fresh_len, first_row, row_count)
    angle_pos = positions.astype(jnp.float32)
    queries = rotate(shaped[:, :, :GROUP], angle_pos).astype(jnp.bfloat16).reshape(row_count, -1)
    new_keys = rotate(shaped[:, :, GROUP], angle_pos).astype(jnp.bfloat16).reshape(row_count, -1)
    new_values = shaped[:, :, GROUP + 1].astype(jnp.bfloat16).reshape(row_count, -1)
    return (queries, new_keys, new_values)


def append_rows(cache, new_rows, cached_len, fresh_len, first_slot):
    slot_count = cache.shape[1]
    slot_pos = first_slot + jnp.arange(slot_count, dtype=jnp.int32)
    offsets = slot_pos[None, :] - cached_len[:, None]
    is_live = (offsets >= 0) & (offsets < fresh_len[:, None])
    source_rows = jnp.arange(REQUESTS, dtype=jnp.int32)[:, None] * NEW_TOKENS + jnp.clip(
        offsets, 0, NEW_TOKENS - 1
    )
    return jnp.where(is_live[:, :, None], jnp.take(new_rows, source_rows, axis=0), cache)


GX = ("y", "zl", "x")
GY = ("zh", "c")


def gather_gx(value):
    for axis in GX[::-1]:
        value = lax.all_gather(value, axis, axis=0, tiled=True)
    return value


def psum_gx(value):
    for axis in GX[::-1]:
        value = lax.psum(value, axis)
    return value


def pmax_gx(value):
    for axis in GX[::-1]:
        value = lax.pmax(value, axis)
    return value


def share_rows(share_sum, cached_len, fresh_len, first_row):
    queries, new_keys, new_values = finish_rows(share_sum, cached_len, fresh_len, first_row)
    widths = (queries.shape[1], new_keys.shape[1])
    joined = gather_gx(jnp.concatenate([queries, new_keys, new_values], axis=1))
    return (
        joined[:, : widths[0]],
        joined[:, widths[0] : widths[0] + widths[1]],
        joined[:, widths[0] + widths[1] :],
    )


def per_device(
    hidden,
    norm_gain,
    qkv_weight,
    qkv_bias,
    out_weight,
    key_cache,
    value_cache,
    cached_len,
    fresh_len,
):
    scale = HEAD_DIM ** (-0.5)
    token_count = REQUESTS * NEW_TOKENS
    gx_size = lax.psum(1, GX)
    model_width = hidden.shape[1] * gx_size
    hidden_f = hidden.astype(jnp.float32)
    squares = psum_gx(jnp.sum(hidden_f * hidden_f, axis=1))
    normed = (
        hidden_f * lax.rsqrt(squares / model_width + NORM_EPS)[:, None] * norm_gain[None, :]
    ).astype(jnp.bfloat16)
    gathered = lax.all_gather(normed, GY, axis=0, tiled=True)
    bias_f = qkv_bias.astype(jnp.float32)[None, :]
    row_share = token_count // gx_size
    share_start = lax.axis_index(GX) * row_share
    summed = lax.psum_scatter(
        jnp.dot(gathered, qkv_weight, preferred_element_type=jnp.float32),
        GX,
        scatter_dimension=0,
        tiled=True,
    )
    queries, new_keys, new_values = share_rows(summed + bias_f, cached_len, fresh_len, share_start)
    slot_count = key_cache.shape[1]
    first_slot = lax.axis_index(GX) * slot_count
    key_out = append_rows(key_cache, new_keys, cached_len, fresh_len, first_slot)
    value_out = append_rows(value_cache, new_values, cached_len, fresh_len, first_slot)
    groups_here = key_cache.shape[2] // HEAD_DIM
    query_blocks = queries.reshape(REQUESTS, NEW_TOKENS, groups_here, GROUP, HEAD_DIM)
    key_blocks = key_out.reshape(REQUESTS, slot_count, groups_here, HEAD_DIM)
    value_blocks = value_out.reshape(REQUESTS, slot_count, groups_here, HEAD_DIM)
    slot_pos = first_slot + jnp.arange(slot_count, dtype=jnp.int32)
    query_pos = jnp.arange(NEW_TOKENS, dtype=jnp.int32)

    def visible_for(cached_here, fresh_here):
        return (slot_pos[None, :] < cached_here + fresh_here) & (
            slot_pos[None, :] <= cached_here + query_pos[:, None]
        )

    def scores_for(query_req, key_req, visible):
        scores = (
            jnp.einsum("ikgd,pkd->kgip", query_req, key_req, preferred_element_type=jnp.float32)
            * scale
        )
        return jnp.where(visible[None, None], scores, NEG_LARGE)

    def local_top(items):
        query_req, key_req, cached_here, fresh_here = items
        return jnp.max(scores_for(query_req, key_req, visible_for(cached_here, fresh_here)), axis=3)

    highest = lax.map(local_top, (query_blocks, key_blocks, cached_len, fresh_len))
    highest = pmax_gx(highest.astype(jnp.bfloat16)).astype(highest.dtype)

    def local_sums(items):
        query_req, key_req, value_req, cached_here, fresh_here, top_here = items
        visible = visible_for(cached_here, fresh_here)
        scores = scores_for(query_req, key_req, visible)
        weighted = jnp.where(visible[None, None], jnp.exp(scores - top_here[..., None]), 0.0)
        denom = jnp.sum(weighted, axis=3)
        mixed = jnp.einsum(
            "kgip,pkd->ikgd",
            weighted.astype(jnp.bfloat16),
            value_req,
            preferred_element_type=jnp.float32,
        )
        return (mixed.reshape(NEW_TOKENS, -1), denom.reshape(-1, NEW_TOKENS).T)

    mixed, denom = lax.map(
        local_sums, (query_blocks, key_blocks, value_blocks, cached_len, fresh_len, highest)
    )
    mixed = mixed.reshape(token_count, -1)
    denom = denom.reshape(token_count, -1)
    mixed_width = mixed.shape[1]
    pad = jnp.zeros((token_count, HEAD_DIM - denom.shape[1]), jnp.float32)
    both = jnp.concatenate([mixed, denom, pad], axis=1).astype(jnp.bfloat16)
    both = lax.psum_scatter(both, GX, scatter_dimension=0, tiled=True).astype(jnp.float32)
    mixed = both[:, :mixed_width]
    denom = both[:, mixed_width : mixed_width + denom.shape[1]]
    unused_pos, is_live = token_positions(cached_len, fresh_len, share_start, row_share)
    ratio = mixed.reshape(row_share, -1, HEAD_DIM) / denom[:, :, None]
    attended = jnp.where(is_live[:, None], ratio.reshape(row_share, -1), 0.0).astype(jnp.bfloat16)
    partial_out = jnp.dot(gather_gx(attended), out_weight, preferred_element_type=jnp.float32)
    summed_out = lax.psum_scatter(
        partial_out.astype(jnp.bfloat16), GY, scatter_dimension=0, tiled=True
    ).astype(jnp.float32)
    output = (hidden_f + summed_out).astype(jnp.bfloat16)
    return (output, key_out, value_out)


def solution(mesh):
    sub_mesh = Mesh(
        mesh.devices.reshape(4, mesh.shape["gx"] // 16, 4, mesh.shape["gy"] // 2, 2), GX + GY
    )
    in_specs = (
        P(GY, GX),
        P(GX),
        P(GX, GY),
        P(GY),
        P(GY, GX),
        P(None, GX, GY),
        P(None, GX, GY),
        P(),
        P(),
    )
    out_specs = (P(GY, GX), P(None, GX, GY), P(None, GX, GY))
    return jax.shard_map(
        per_device, mesh=sub_mesh, in_specs=in_specs, out_specs=out_specs, check_vma=False
    )
```

profile of v0, /device:TPU:10, one launch (start us, length us, event | category | flops | bytes accessed | tf_op | source)
XLA Modules:
  0.0 617.7 jit_solution(14488319229614992455)
XLA Ops:
  8.2 8.6 %psum.21 = f32[280]{0:T(512)S(1)} all-reduce(f32[280]{0:T(512)S(1)} %fusion.40), channel_id=1, replica_groups=mesh['y'=4,'zl'=2,'x'=4,'zh'=4,'c'=2] {'x'}, use_global_device_ids=true, to_apply=%region_2.0 | all-reduce | flops 280 | bytes 2240 | tf_op jit(solution)/shard_map/psum | solution.py:80
  16.8 4.9 psum.22
  21.7 9.5 %psum.23 = f32[280]{0:T(512)S(1)} all-reduce(f32[280]{0:T(512)S(1)} %psum.22), channel_id=1, replica_groups=mesh['y'=4,'zl'=2,'x'=4,'zh'=4,'c'=2] {'y'}, use_global_device_ids=true, to_apply=%region_4.0 | all-reduce | flops 280 | bytes 2240 | tf_op jit(solution)/shard_map/psum | solution.py:80
  32.2 19.2 %all-gather = bf16[8,280,160]{1,2,0:T(8,128)(2,1)S(1)} all-gather(bf16[1,280,160]{1,2,0:T(8,128)(2,1)S(1)} %fusion.46), channel_id=1, replica_groups=mesh['y'=4,'zl'=2,'x'=4,'zh'=4,'c'=2] {'zh','c'}, dimensions={0}, use_global_device_ids=true | all-gather | bytes 806400 | tf_op jit(solution)/shard_map/all_gather | solution.py:121
  52.5 4.5 fusion.63
  57.0 115.8 %fusion.8 = f32[80,896]{1,0:T(8,128)S(1)} fusion(f32[2240,896]{1,0:T(8,128)} %fusion.63), kind=kCustom, calls=%all-reduce-scatter | all-reduce-scatter fusion | flops 2293761 | bytes 8315904
  172.8 2.1 collective-permute-start
  175.0 3.4 collective-permute-start.1
  178.4 5.2 collective-permute-start.2
  183.7 3.5 collective-permute-start.3
  189.4 8.7 %collective-permute-done.3 = f32[70,896]{1,0:T(8,128)S(1)} collective-permute-done((f32[70,896]{1,0:T(8,128)S(1)}, f32[70,896]{1,0:T(8,128)S(1)}, u32[]{:S(2)}, u32[]{:S(2)}) %collective-permute-start.3) | collective-permute-done | bytes 250912
  200.4 14.4 %all-gather.1 = bf16[4,70,896]{2,1,0:T(8,128)(2,1)S(1)} all-gather(bf16[1,70,896]{2,1,0:T(8,128)(2,1)S(1)} %maximum_bitcast_fusion.1), channel_id=1, replica_groups=mesh['y'=4,'zl'=2,'x'=4,'zh'=4,'c'=2] {'x'}, dimensions={0}, use_global_device_ids=true | all-gather | bytes 627200 | tf_op jit(solution)/shard_map/all_gather | solution.py:74
  215.0 9.7 %all_gather.23 = bf16[560,896]{1,0:T(8,128)(2,1)} all-gather(bf16[280,896]{1,0:T(8,128)(2,1)S(1)} %reshape.471), channel_id=1, replica_groups=mesh['y'=4,'zl'=2,'x'=4,'zh'=4,'c'=2] {'zl'}, dimensions={0}, use_global_device_ids=true | all-gather | bytes 1505280 | tf_op jit(solution)/shard_map/all_gather | solution.py:74
  225.1 46.4 %all-gather.6.cloned.1.call-done = bf16[2240,896]{1,0:T(8,128)(2,1)} async-done(((bf16[560,896]{1,0:T(8,128)(2,1)}), bf16[2240,896]{1,0:T(8,128)(2,1)}) %all-gather.6.cloned.1.call-update) | async-done | bytes 4014096 | tf_op jit(solution)/shard_map/all_gather | solution.py:74
  271.5 1.8 slice-done
  273.3 5.2 reshape.445
  278.5 4.8 copy.68
  283.4 3.3 gather_fusion
  286.8 3.3 gather_fusion.1
  290.7 24.8 %while.24 = (s32[]{:T(128)}, bf16[5,1,5,448]{3,2,1,0:T(8,128)(2,1)S(1)}, s32[5]{0:T(128)S(1)}, s32[5]{0:T(128)S(1)}, bf16[5,272,1,128]{3,1,2,0:T(8,128)(2,1)S(1)...) while((s32[]{:T(128)}, bf16[5,1,5,448]{3,2,1,0:T(8,128)(2,1)S(1)}, ...), condition=%wide.region_9.11_spmd.clone, body=%wide.region_7.10_spmd.clone.sunk | while | flops 158046256 | bytes 932525 | solution.py:159
  294.0 1.7 fusion.77
  298.9 1.7 fusion.77
  303.9 1.7 fusion.77
  308.8 1.7 fusion.77
  313.8 1.7 fusion.77
  315.5 14.4 %pmax.21 = bf16[5,1,5,448]{3,2,1,0:T(8,128)(2,1)S(1)} all-reduce(bf16[5,1,5,448]{3,2,1,0:T(8,128)(2,1)S(1)} %get-tuple-element.104), channel_id=1, replica_groups=mesh['y'=4,'zl'=2,'x'=4,'zh'=4,'c'=2] {'x'}, use_global_device_ids=true, to_apply=%region_10.12 | all-reduce | flops 11200 | bytes 44800 | tf_op jit(solution)/shard_map/pmax | solution.py:86
  329.9 8.5 %pmax.22 = bf16[5,1,5,448]{3,2,1,0:T(8,128)(2,1)S(1)} all-reduce(bf16[5,1,5,448]{3,2,1,0:T(8,128)(2,1)S(1)} %pmax.21), channel_id=1, replica_groups=mesh['y'=4,'zl'=2,'x'=4,'zh'=4,'c'=2] {'zl'}, use_global_device_ids=true, to_apply=%region_11.13 | all-reduce | flops 11200 | bytes 44800 | tf_op jit(solution)/shard_map/pmax | solution.py:86
  338.5 14.7 %pmax.23 = bf16[5,1,5,448]{3,2,1,0:T(8,128)(2,1)S(1)} all-reduce(bf16[5,1,5,448]{3,2,1,0:T(8,128)(2,1)S(1)} %pmax.22), channel_id=1, replica_groups=mesh['y'=4,'zl'=2,'x'=4,'zh'=4,'c'=2] {'y'}, use_global_device_ids=true, to_apply=%region_12.14 | all-reduce | flops 11200 | bytes 44800 | tf_op jit(solution)/shard_map/pmax | solution.py:86
  353.2 38.3 %while.25 = (s32[]{:T(128)}, bf16[5,448,640]{1,2,0:T(8,128)(2,1)}, bf16[5,448,5]{1,2,0:T(8,128)(2,1)S(1)}, bf16[5,272,1,128]{3,1,2,0:T(8,128)(2,1)S(1)}, s32[5]{...) while((s32[]{:T(128)}, bf16[5,448,640]{1,2,0:T(8,128)(2,1)}, ...), condition=%wide.region_15.17_spmd.clone, body=%wide.region_13.16_spmd.clone.sunk | while | flops 318286912 | bytes 9364173 | solution.py:176
  356.4 2.1 fusion.80
  358.6 1.1 fusion.81
  364.2 2.1 fusion.80
  366.3 1.1 fusion.81
  371.8 2.1 fusion.80
  379.4 2.1 fusion.80
  381.6 1.1 fusion.81
  387.1 2.1 fusion.80
  392.3 4.3 copy.69
  397.7 3.5 maximum_maximum_fusion
  401.2 88.4 %fusion.9 = bf16[72,768]{1,0:T(8,128)(2,1)S(1)} fusion(bf16[2240,768]{1,0:T(8,128)(2,1)} %maximum_maximum_fusion), kind=kCustom, calls=%all-reduce-scatter.1 | all-reduce-scatter fusion | flops 1769473 | bytes 3552256
  489.7 2.1 collective-permute-start.4
  492.4 3.9 collective-permute-done.4
  496.9 15.3 %all-gather.2 = bf16[4,70,640]{2,1,0:T(8,128)(2,1)S(1)} all-gather(bf16[1,70,640]{2,1,0:T(8,128)(2,1)S(1)} %fusion.47), channel_id=1, replica_groups=mesh['y'=4,'zl'=2,'x'=4,'zh'=4,'c'=2] {'x'}, dimensions={0}, use_global_device_ids=true | all-gather | bytes 448000 | tf_op jit(solution)/shard_map/all_gather | solution.py:74
  512.3 8.2 %all_gather.26 = bf16[560,640]{1,0:T(8,128)(2,1)} all-gather(bf16[280,640]{1,0:T(8,128)(2,1)S(1)} %reshape.473), channel_id=1, replica_groups=mesh['y'=4,'zl'=2,'x'=4,'zh'=4,'c'=2] {'zl'}, dimensions={0}, use_global_device_ids=true | all-gather | bytes 1075200 | tf_op jit(solution)/shard_map/all_gather | solution.py:74
  520.6 43.0 %all-gather.8.cloned.1.call-done = bf16[2240,640]{1,0:T(8,128)(2,1)} async-done(((bf16[560,640]{1,0:T(8,128)(2,1)}), bf16[2240,640]{1,0:T(8,128)(2,1)}) %all-gather.8.cloned.1.call-update) | async-done | bytes 2867216 | tf_op jit(solution)/shard_map/all_gather | solution.py:74
  563.6 2.8 convolution_convert_fusion
  566.4 1.5 copy.73
  567.9 41.5 %reduce-scatter.8.cloned.1.call-done = bf16[280,160]{1,0:T(8,128)(2,1)} async-done(((bf16[2240,160]{1,0:T(8,128)(2,1)}), bf16[280,160]{1,0:T(8,128)(2,1)}) %reduce-scatter.8.cloned.1.call-update) | async-done | bytes 89616
  (185 shorter events, 40.3 us)
Async XLA Ops:
  7.2 45.3 %copy-start = (bf16[160,896]{1,0:T(8,128)(2,1)S(1)}, bf16[160,896]{1,0:T(8,128)(2,1)}, u32[]{:S(2)}) copy-start(bf16[160,896]{1,0:T(8,128)(2,1)} %param.17) | copy-start | bytes 860164
  7.2 264.3 %all-gather.6.cloned.1.call-start = ((), (), s32[]{:S(2)}) async-start(), calls=%async_computation.1 | async-start | bytes 5017600 | tf_op jit(solution)/shard_map/all_gather | solution.py:74
  57.0 130.1 %copy-start.9 = (s32[5]{0:T(128)S(1)}, s32[5]{0:T(128)}, u32[]{:S(2)}) copy-start(s32[5]{0:T(128)} %param.22) | copy-start | bytes 64
  57.0 130.1 %copy-start.12 = (s32[5]{0:T(128)S(1)}, s32[5]{0:T(128)}, u32[]{:S(2)}) copy-start(s32[5]{0:T(128)} %param.23) | copy-start | bytes 64
  57.0 130.9 %copy-start.11 = (bf16[896]{0:T(1024)(128)(2,1)S(1)}, bf16[896]{0:T(1024)(128)(2,1)}, u32[]{:S(2)}) copy-start(bf16[896]{0:T(1024)(128)(2,1)} %param.18) | copy-start | bytes 5380
  57.0 130.9 %copy-start.15 = (u32[256]{0:T(256)S(1)}, u32[256]{0:T(256)}, u32[]{:S(2)}) copy-start(u32[256]{0:T(256)} %constant.122) | copy-start | bytes 3076
  172.8 25.3 %collective-permute-start = (f32[80,896]{1,0:T(8,128)S(1)}, f32[80,896]{1,0:T(8,128)S(1)}, u32[]{:S(2)}, u32[]{:S(2)}) collective-permute-start(f32[80,896]{1,0:T(8,128)S(1)} %fusion.8), channel_id=1, source_target_pairs={{0,8},{8,16},{16,24},{24,32},{32,40},{40,48},{48,56},{56,64},{64,7... | collective-permute-start | bytes 860168
  175.0 23.2 %collective-permute-start.1 = (f32[80,896]{1,0:T(8,128)S(1)}, f32[80,896]{1,0:T(8,128)S(1)}, u32[]{:S(2)}, u32[]{:S(2)}) collective-permute-start(f32[80,896]{1,0:T(8,128)S(1)} %fusion.8), channel_id=1, source_target_pairs={{0,16},{8,24},{16,32},{24,40},{32,48},{40,56},{48,64},{56,72},{64,... | collective-permute-start | bytes 860168
  178.4 19.7 %collective-permute-start.2 = (f32[80,896]{1,0:T(8,128)S(1)}, f32[80,896]{1,0:T(8,128)S(1)}, u32[]{:S(2)}, u32[]{:S(2)}) collective-permute-start(f32[80,896]{1,0:T(8,128)S(1)} %fusion.8), channel_id=1, source_target_pairs={{0,24},{8,32},{16,40},{24,48},{32,56},{40,64},{48,72},{56,80},{64,... | collective-permute-start | bytes 860168
  183.7 14.5 %collective-permute-start.3 = (f32[70,896]{1,0:T(8,128)S(1)}, f32[70,896]{1,0:T(8,128)S(1)}, u32[]{:S(2)}, u32[]{:S(2)}) collective-permute-start(f32[70,896]{1,0:T(8,128)S(1)} %slice.63), channel_id=1, source_target_pairs={{0,32},{8,40},{16,48},{24,56},{32,64},{40,72},{48,80},{56,88},{64,... | collective-permute-start | bytes 752648
  224.7 338.9 %all-gather.8.cloned.1.call-start = ((), (), s32[]{:S(2)}) async-start(), calls=%async_computation.2 | async-start | bytes 3584000 | tf_op jit(solution)/shard_map/all_gather | solution.py:74
  271.5 1.8 slice-start
  278.5 4.8 copy-start.1
  283.4 6.7 %copy-start.3 = (bf16[5,272,128]{2,1,0:T(8,128)(2,1)S(1)}, bf16[5,272,128]{2,1,0:T(8,128)(2,1)}, u32[]{:S(2)}) copy-start(bf16[5,272,128]{2,1,0:T(8,128)(2,1)} %param.20) | copy-start | bytes 1044484
  283.4 6.7 %copy-start.4 = (bf16[5,272,128]{2,1,0:T(8,128)(2,1)S(1)}, bf16[5,272,128]{2,1,0:T(8,128)(2,1)}, u32[]{:S(2)}) copy-start(bf16[5,272,128]{2,1,0:T(8,128)(2,1)} %param.21) | copy-start | bytes 1044484
  286.7 4.0 copy-start.8
  286.8 4.0 copy-start.10
  286.8 4.0 copy-start.13
  391.5 0.7 copy-start.6
  392.3 4.3 copy-start.5
  401.2 90.5 %copy-start.14 = (s32[70]{0:T(128)S(1)}, s32[70]{0:T(128)}, u32[]{:S(2)}) copy-start(s32[70]{0:T(128)} %get-tuple-element.234) | copy-start | bytes 844
  489.6 74.0 %copy-start.7 = (bf16[640,160]{0,1:T(8,128)(2,1)S(1)}, bf16[640,160]{0,1:T(8,128)(2,1)}, u32[]{:S(2)}) copy-start(bf16[640,160]{0,1:T(8,128)(2,1)} %param.19) | copy-start | bytes 614404
  489.7 6.6 %collective-permute-start.4 = (bf16[62,768]{1,0:T(8,128)(2,1)S(1)}, bf16[62,768]{1,0:T(8,128)(2,1)S(1)}, u32[]{:S(2)}, u32[]{:S(2)}) collective-permute-start(bf16[62,768]{1,0:T(8,128)(2,1)S(1)} %slice.64), channel_id=1, source_target_pairs={{0,8},{8,16},{16,24},{24,32},{32,40},{40,48},{48,56},{56,64},{64,7... | collective-permute-start | bytes 285704
  520.5 88.9 %reduce-scatter.8.cloned.1.call-start = ((), (), s32[]{:S(2)}) async-start(), calls=%async_computation.3 | async-start | bytes 1290240
  566.4 44.0 %copy-start.2 = (bf16[280,160]{0,1:T(8,128)(2,1)S(1)}, bf16[280,160]{0,1:T(8,128)(2,1)}, u32[]{:S(2)}) copy-start(bf16[280,160]{0,1:T(8,128)(2,1)} %param.15) | copy-start | bytes 268804
Sparse Core Ops, SparseCore 0:
  224.8 46.6 all-gather.5
  520.7 42.8 all-gather.7
  568.0 41.3 reduce-scatter.7
where the time goes:
time: 619 us; the launch traced here: 618 us
  blocking collectives  332 us (54%)
  waiting for transfers between devices  144 us (23%)
  local copies, waits for them, and re-layouts  48.8 us (8%)
  matrix products  32.1 us (5%)
  other arithmetic  16.9 us (3%)
  starting transfers between devices  16.4 us (3%)
  between operations  15.6 us (3%)
  loops' own time  12.7 us (2%)
    unnamed x2, blocking collectives  204 us
    all_gather x2, waiting for transfers between devices, gather_gx(): value = lax.all_gather(value, axis, axis=0, tiled=True)  89.4 us
    unnamed x9, waiting for transfers between devices  54.2 us
    all_gather x4, blocking collectives, gather_gx(): value = lax.all_gather(value, axis, axis=0, tiled=True)  47.6 us
    pmax x3, blocking collectives, pmax_gx(): value = lax.pmax(value, axis)  37.6 us
    psum x3, blocking collectives, psum_gx(): value = lax.psum(value, axis)  23 us
    dot_general x10, matrix products, scores_for(): jnp.einsum('ikgd,pkd->kgip', query_req, key_req, preferred_element_type=j...  19.2 us
    all_gather x1, blocking collectives, per_device(): gathered = lax.all_gather(normed, GY, axis=0, tiled=True)  19.2 us
  transfers between devices with their start and end apart: 8, of which 5 were waited for; matrix products, arithmetic and copies ran while one was open for 0% of the time, Pallas kernels for 0%

commit v1 on v0

--- a/solution.py
+++ b/solution.py
@@ -11,6 +11,10 @@
 ROPE_THETA = 1000000.0
 NORM_EPS = 1e-06
 NEG_LARGE = -1e30
+
+
+def part_yards_for(inp, a_name):
+    return lax.all_gather(inp, a_name).sum(axis=0)
 
 
 def rotate(vectors, positions):
@@ -77,7 +81,7 @@
 
 def psum_gx(value):
     for axis in GX[::-1]:
-        value = lax.psum(value, axis)
+        value = part_yards_for(value, axis)
     return value
 
 

time: 619 us -> 628 us (1.015)
    unnamed x2 -> x5, blocking collectives: 204 us -> 227 us
    psum x3 -> x0, blocking collectives: 23 us -> none  [psum_gx(): value = lax.psum(value, axis)]
    unnamed x49 -> x58, local copies, waits for them, and re-layouts: 11.2 us -> 15.9 us
where the time goes in v1:
time: 628 us; the launch traced here: 626 us
  blocking collectives  332 us (53%)
  waiting for transfers between devices  143 us (23%)
  local copies, waits for them, and re-layouts  54.6 us (9%)
  matrix products  32.1 us (5%)
  between operations  17.7 us (3%)
  other arithmetic  16.9 us (3%)
  starting transfers between devices  16.5 us (3%)
  loops' own time  14 us (2%)
    unnamed x5, blocking collectives  227 us
    all_gather x2, waiting for transfers between devices, gather_gx(): value = lax.all_gather(value, axis, axis=0, tiled=True)  88.9 us
    unnamed x9, waiting for transfers between devices  53.8 us
    all_gather x4, blocking collectives, gather_gx(): value = lax.all_gather(value, axis, axis=0, tiled=True)  47.7 us
    pmax x3, blocking collectives, pmax_gx(): value = lax.pmax(value, axis)  37.6 us
    dot_general x10, matrix products, scores_for(): jnp.einsum('ikgd,pkd->kgip', query_req, key_req, preferred_element_type=j...  19.2 us
    all_gather x1, blocking collectives, per_device(): gathered = lax.all_gather(normed, GY, axis=0, tiled=True)  19.2 us
    unnamed x6, starting transfers between devices  16.4 us
  transfers between devices with their start and end apart: 8, of which 5 were waited for; matrix products, arithmetic and copies ran while one was open for 0% of the time, Pallas kernels for 0%

profile of v1, /device:TPU:10, one launch (start us, length us, event | category | flops | bytes accessed | tf_op | source)
XLA Modules:
  0.0 626.5 jit_solution(1323620775198033264)
XLA Ops:
  8.2 1.3 dynamic-slice
  10.4 8.7 %all-reduce = f32[1120]{0:T(1024)S(1)} all-reduce(f32[1120]{0:T(1024)S(1)} %dynamic-update-slice), channel_id=2, replica_groups=mesh['y'=4,'zl'=2,'x'=4,'zh'=4,'c'=2] {'x'}, use_global_device_ids=true, to_apply=%add | all-reduce | flops 1120 | bytes 8960
  19.2 1.3 dynamic-slice.1
  21.4 4.9 all-reduce.1
  26.4 1.3 dynamic-slice.2
  28.6 9.6 %all-reduce.2 = f32[1120]{0:T(1024)S(1)} all-reduce(f32[1120]{0:T(1024)S(1)} %dynamic-update-slice.2), channel_id=4, replica_groups=mesh['y'=4,'zl'=2,'x'=4,'zh'=4,'c'=2] {'y'}, use_global_device_ids=true, to_apply=%add.2 | all-reduce | flops 1120 | bytes 8960
  39.4 19.2 %all-gather.3 = bf16[8,280,160]{1,2,0:T(8,128)(2,1)S(1)} all-gather(bf16[1,280,160]{1,2,0:T(8,128)(2,1)S(1)} %fusion.46), channel_id=1, replica_groups=mesh['y'=4,'zl'=2,'x'=4,'zh'=4,'c'=2] {'zh','c'}, dimensions={0}, use_global_device_ids=true | all-gather | bytes 806400 | tf_op jit(solution)/shard_map/all_gather | solution.py:125
  59.6 4.5 fusion.63
  64.1 115.8 %fusion.8 = f32[80,896]{1,0:T(8,128)S(1)} fusion(f32[2240,896]{1,0:T(8,128)} %fusion.63), kind=kCustom, calls=%all-reduce-scatter | all-reduce-scatter fusion | flops 2293761 | bytes 8315904
  179.9 2.1 collective-permute-start
  182.1 3.4 collective-permute-start.1
  185.5 5.3 collective-permute-start.2
  190.8 3.5 collective-permute-start.3
  196.7 8.5 %collective-permute-done.3 = f32[70,896]{1,0:T(8,128)S(1)} collective-permute-done((f32[70,896]{1,0:T(8,128)S(1)}, f32[70,896]{1,0:T(8,128)S(1)}, u32[]{:S(2)}, u32[]{:S(2)}) %collective-permute-start.3) | collective-permute-done | bytes 250912
  207.4 14.5 %all-gather.4 = bf16[4,70,896]{2,1,0:T(8,128)(2,1)S(1)} all-gather(bf16[1,70,896]{2,1,0:T(8,128)(2,1)S(1)} %maximum_bitcast_fusion.1), channel_id=1, replica_groups=mesh['y'=4,'zl'=2,'x'=4,'zh'=4,'c'=2] {'x'}, dimensions={0}, use_global_device_ids=true | all-gather | bytes 627200 | tf_op jit(solution)/shard_map/all_gather | solution.py:78
  222.1 9.7 %all_gather.47 = bf16[560,896]{1,0:T(8,128)(2,1)} all-gather(bf16[280,896]{1,0:T(8,128)(2,1)S(1)} %reshape.487), channel_id=1, replica_groups=mesh['y'=4,'zl'=2,'x'=4,'zh'=4,'c'=2] {'zl'}, dimensions={0}, use_global_device_ids=true | all-gather | bytes 1505280 | tf_op jit(solution)/shard_map/all_gather | solution.py:78
  232.3 45.9 %all-gather.9.cloned.1.call-done = bf16[2240,896]{1,0:T(8,128)(2,1)} async-done(((bf16[560,896]{1,0:T(8,128)(2,1)}), bf16[2240,896]{1,0:T(8,128)(2,1)}) %all-gather.9.cloned.1.call-update) | async-done | bytes 4014096 | tf_op jit(solution)/shard_map/all_gather | solution.py:78
  278.2 1.8 slice-done
  280.0 5.2 reshape.449
  285.2 4.8 copy.68
  290.1 3.3 gather_fusion
  293.4 3.3 gather_fusion.1
  297.4 25.9 %while.24 = (s32[]{:T(128)}, bf16[5,1,5,448]{3,2,1,0:T(8,128)(2,1)S(1)}, s32[5]{0:T(128)S(1)}, s32[5]{0:T(128)S(1)}, bf16[5,272,1,128]{3,1,2,0:T(8,128)(2,1)S(1)...) while((s32[]{:T(128)}, bf16[5,1,5,448]{3,2,1,0:T(8,128)(2,1)S(1)}, ...), condition=%wide.region_9.11_spmd.clone, body=%wide.region_7.10_spmd.clone.sunk | while | flops 158046256 | bytes 932525 | solution.py:163
  300.8 1.7 fusion.77
  306.0 1.7 fusion.77
  311.2 1.7 fusion.77
  316.4 1.7 fusion.77
  321.5 1.7 fusion.77
  323.3 14.4 %pmax.21 = bf16[5,1,5,448]{3,2,1,0:T(8,128)(2,1)S(1)} all-reduce(bf16[5,1,5,448]{3,2,1,0:T(8,128)(2,1)S(1)} %get-tuple-element.104), channel_id=1, replica_groups=mesh['y'=4,'zl'=2,'x'=4,'zh'=4,'c'=2] {'x'}, use_global_device_ids=true, to_apply=%region_10.12 | all-reduce | flops 11200 | bytes 44800 | tf_op jit(solution)/shard_map/pmax | solution.py:90
  337.7 8.6 %pmax.22 = bf16[5,1,5,448]{3,2,1,0:T(8,128)(2,1)S(1)} all-reduce(bf16[5,1,5,448]{3,2,1,0:T(8,128)(2,1)S(1)} %pmax.21), channel_id=1, replica_groups=mesh['y'=4,'zl'=2,'x'=4,'zh'=4,'c'=2] {'zl'}, use_global_device_ids=true, to_apply=%region_11.13 | all-reduce | flops 11200 | bytes 44800 | tf_op jit(solution)/shard_map/pmax | solution.py:90
  346.2 14.7 %pmax.23 = bf16[5,1,5,448]{3,2,1,0:T(8,128)(2,1)S(1)} all-reduce(bf16[5,1,5,448]{3,2,1,0:T(8,128)(2,1)S(1)} %pmax.22), channel_id=1, replica_groups=mesh['y'=4,'zl'=2,'x'=4,'zh'=4,'c'=2] {'y'}, use_global_device_ids=true, to_apply=%region_12.14 | all-reduce | flops 11200 | bytes 44800 | tf_op jit(solution)/shard_map/pmax | solution.py:90
  361.0 39.4 %while.25 = (s32[]{:T(128)}, bf16[5,448,640]{1,2,0:T(8,128)(2,1)}, bf16[5,448,5]{1,2,0:T(8,128)(2,1)S(1)}, bf16[5,272,1,128]{3,1,2,0:T(8,128)(2,1)S(1)}, s32[5]{...) while((s32[]{:T(128)}, bf16[5,448,640]{1,2,0:T(8,128)(2,1)}, ...), condition=%wide.region_15.17_spmd.clone, body=%wide.region_13.16_spmd.clone.sunk | while | flops 318286912 | bytes 9364173 | solution.py:180
  364.4 2.1 fusion.80
  372.3 2.1 fusion.80
  380.2 2.1 fusion.80
  388.1 2.1 fusion.80
  396.0 2.1 fusion.80
  401.1 4.3 copy.69
  406.6 3.5 maximum_maximum_fusion
  410.1 88.4 %fusion.9 = bf16[72,768]{1,0:T(8,128)(2,1)S(1)} fusion(bf16[2240,768]{1,0:T(8,128)(2,1)} %maximum_maximum_fusion), kind=kCustom, calls=%all-reduce-scatter.1 | all-reduce-scatter fusion | flops 1769473 | bytes 3552256
  498.6 2.1 collective-permute-start.4
  501.4 3.9 collective-permute-done.4
  505.8 15.3 %all-gather.5 = bf16[4,70,640]{2,1,0:T(8,128)(2,1)S(1)} all-gather(bf16[1,70,640]{2,1,0:T(8,128)(2,1)S(1)} %fusion.47), channel_id=1, replica_groups=mesh['y'=4,'zl'=2,'x'=4,'zh'=4,'c'=2] {'x'}, dimensions={0}, use_global_device_ids=true | all-gather | bytes 448000 | tf_op jit(solution)/shard_map/all_gather | solution.py:78
  521.2 8.2 %all_gather.50 = bf16[560,640]{1,0:T(8,128)(2,1)} all-gather(bf16[280,640]{1,0:T(8,128)(2,1)S(1)} %reshape.489), channel_id=1, replica_groups=mesh['y'=4,'zl'=2,'x'=4,'zh'=4,'c'=2] {'zl'}, dimensions={0}, use_global_device_ids=true | all-gather | bytes 1075200 | tf_op jit(solution)/shard_map/all_gather | solution.py:78
  529.5 43.1 %all-gather.11.cloned.1.call-done = bf16[2240,640]{1,0:T(8,128)(2,1)} async-done(((bf16[560,640]{1,0:T(8,128)(2,1)}), bf16[2240,640]{1,0:T(8,128)(2,1)}) %all-gather.11.cloned.1.call-update) | async-done | bytes 2867216 | tf_op jit(solution)/shard_map/all_gather | solution.py:78
  572.5 2.8 convolution_convert_fusion
  575.3 1.5 copy.73
  576.8 41.4 %reduce-scatter.8.cloned.1.call-done = bf16[280,160]{1,0:T(8,128)(2,1)} async-done(((bf16[2240,160]{1,0:T(8,128)(2,1)}), bf16[280,160]{1,0:T(8,128)(2,1)}) %reduce-scatter.8.cloned.1.call-update) | async-done | bytes 89616
  (200 shorter events, 45.7 us)
Async XLA Ops:
  7.2 52.5 %copy-start = (bf16[160,896]{1,0:T(8,128)(2,1)S(1)}, bf16[160,896]{1,0:T(8,128)(2,1)}, u32[]{:S(2)}) copy-start(bf16[160,896]{1,0:T(8,128)(2,1)} %param.17) | copy-start | bytes 860164
  7.2 271.0 %all-gather.9.cloned.1.call-start = ((), (), s32[]{:S(2)}) async-start(), calls=%async_computation.1 | async-start | bytes 5017600 | tf_op jit(solution)/shard_map/all_gather | solution.py:78
  64.1 130.2 %copy-start.9 = (s32[5]{0:T(128)S(1)}, s32[5]{0:T(128)}, u32[]{:S(2)}) copy-start(s32[5]{0:T(128)} %param.22) | copy-start | bytes 64
  64.1 130.2 %copy-start.12 = (s32[5]{0:T(128)S(1)}, s32[5]{0:T(128)}, u32[]{:S(2)}) copy-start(s32[5]{0:T(128)} %param.23) | copy-start | bytes 64
  64.1 130.9 %copy-start.11 = (bf16[896]{0:T(1024)(128)(2,1)S(1)}, bf16[896]{0:T(1024)(128)(2,1)}, u32[]{:S(2)}) copy-start(bf16[896]{0:T(1024)(128)(2,1)} %param.18) | copy-start | bytes 5380
  64.1 130.9 %copy-start.15 = (u32[256]{0:T(256)S(1)}, u32[256]{0:T(256)}, u32[]{:S(2)}) copy-start(u32[256]{0:T(256)} %constant.140) | copy-start | bytes 3076
  179.9 25.2 %collective-permute-start = (f32[80,896]{1,0:T(8,128)S(1)}, f32[80,896]{1,0:T(8,128)S(1)}, u32[]{:S(2)}, u32[]{:S(2)}) collective-permute-start(f32[80,896]{1,0:T(8,128)S(1)} %fusion.8), channel_id=1, source_target_pairs={{0,8},{8,16},{16,24},{24,32},{32,40},{40,48},{48,56},{56,64},{64,7... | collective-permute-start | bytes 860168
  182.1 23.1 %collective-permute-start.1 = (f32[80,896]{1,0:T(8,128)S(1)}, f32[80,896]{1,0:T(8,128)S(1)}, u32[]{:S(2)}, u32[]{:S(2)}) collective-permute-start(f32[80,896]{1,0:T(8,128)S(1)} %fusion.8), channel_id=1, source_target_pairs={{0,16},{8,24},{16,32},{24,40},{32,48},{40,56},{48,64},{56,72},{64,... | collective-permute-start | bytes 860168
  185.5 19.7 %collective-permute-start.2 = (f32[80,896]{1,0:T(8,128)S(1)}, f32[80,896]{1,0:T(8,128)S(1)}, u32[]{:S(2)}, u32[]{:S(2)}) collective-permute-start(f32[80,896]{1,0:T(8,128)S(1)} %fusion.8), channel_id=1, source_target_pairs={{0,24},{8,32},{16,40},{24,48},{32,56},{40,64},{48,72},{56,80},{64,... | collective-permute-start | bytes 860168
  190.8 14.3 %collective-permute-start.3 = (f32[70,896]{1,0:T(8,128)S(1)}, f32[70,896]{1,0:T(8,128)S(1)}, u32[]{:S(2)}, u32[]{:S(2)}) collective-permute-start(f32[70,896]{1,0:T(8,128)S(1)} %slice.63), channel_id=1, source_target_pairs={{0,32},{8,40},{16,48},{24,56},{32,64},{40,72},{48,80},{56,88},{64,... | collective-permute-start | bytes 752648
  231.9 340.6 %all-gather.11.cloned.1.call-start = ((), (), s32[]{:S(2)}) async-start(), calls=%async_computation.2 | async-start | bytes 3584000 | tf_op jit(solution)/shard_map/all_gather | solution.py:78
  278.2 1.8 slice-start
  285.2 4.8 copy-start.1
  290.1 6.7 %copy-start.3 = (bf16[5,272,128]{2,1,0:T(8,128)(2,1)S(1)}, bf16[5,272,128]{2,1,0:T(8,128)(2,1)}, u32[]{:S(2)}) copy-start(bf16[5,272,128]{2,1,0:T(8,128)(2,1)} %param.20) | copy-start | bytes 1044484
  290.1 6.7 %copy-start.4 = (bf16[5,272,128]{2,1,0:T(8,128)(2,1)S(1)}, bf16[5,272,128]{2,1,0:T(8,128)(2,1)}, u32[]{:S(2)}) copy-start(bf16[5,272,128]{2,1,0:T(8,128)(2,1)} %param.21) | copy-start | bytes 1044484
  293.4 4.0 copy-start.8
  293.4 4.0 copy-start.10
  293.4 4.0 copy-start.13
  400.4 0.7 copy-start.6
  401.1 4.3 copy-start.5
  410.1 90.5 %copy-start.14 = (s32[70]{0:T(128)S(1)}, s32[70]{0:T(128)}, u32[]{:S(2)}) copy-start(s32[70]{0:T(128)} %get-tuple-element.234) | copy-start | bytes 844
  498.6 73.9 %copy-start.7 = (bf16[640,160]{0,1:T(8,128)(2,1)S(1)}, bf16[640,160]{0,1:T(8,128)(2,1)}, u32[]{:S(2)}) copy-start(bf16[640,160]{0,1:T(8,128)(2,1)} %param.19) | copy-start | bytes 614404
  498.6 6.6 %collective-permute-start.4 = (bf16[62,768]{1,0:T(8,128)(2,1)S(1)}, bf16[62,768]{1,0:T(8,128)(2,1)S(1)}, u32[]{:S(2)}, u32[]{:S(2)}) collective-permute-start(bf16[62,768]{1,0:T(8,128)(2,1)S(1)} %slice.64), channel_id=1, source_target_pairs={{0,8},{8,16},{16,24},{24,32},{32,40},{40,48},{48,56},{56,64},{64,7... | collective-permute-start | bytes 285704
  529.4 88.8 %reduce-scatter.8.cloned.1.call-start = ((), (), s32[]{:S(2)}) async-start(), calls=%async_computation.3 | async-start | bytes 1290240
  575.3 43.9 %copy-start.2 = (bf16[280,160]{0,1:T(8,128)(2,1)S(1)}, bf16[280,160]{0,1:T(8,128)(2,1)}, u32[]{:S(2)}) copy-start(bf16[280,160]{0,1:T(8,128)(2,1)} %param.15) | copy-start | bytes 268804
Sparse Core Ops, SparseCore 0:
  232.0 46.1 all-gather.8
  529.5 42.9 all-gather.10
  576.9 41.2 reduce-scatter.7
